TPU v7x, 256 devices: a whole 4x4x8 slice. The times are simulated.
256 devices in a mesh: tm: 64 (over x, z, core), space: 4 (over y).
Axes of the slice: x: 4, y: 4, z: 8, core: 2. Of those that a mesh axis runs over, the one named last changes fastest.
Arguments:
- snapshots: float32 [4096, 16384], P('tm', 'space'), as said below
- space_factor: float32 [16384, 256], P('space'), as said below
Outputs:
- time_factor: float32 [4096, 256], P('tm')
- loadings: float32 [256, 16384], P('tm', 'space')
Inputs may be any that keep to these rules, and one draw needn't show every extreme that they name: `snapshots`: entries are real values. `space_factor`: entries are real values; columns have norms between 0.05 and 1, the previous sweep's singular values.
All inputs are finite; a program needn't handle non-finite values.
Results may differ from a plain program's by a relative error of at most 0.0001.
Values sent between devices are 32-bit elements; how exact they have to be, the bound alone decides.
A program may use at most 64 MiB of HBM per device.

v0:
```python
import math
import jax
import jax.numpy as jnp
from jax import lax
from jax.sharding import PartitionSpec as P

RANK = 256
NS = 2


def inner(left, right):
    return lax.dot_general(
        left,
        right,
        (((0,), (0,)), ((), ())),
        precision=lax.Precision.HIGHEST,
        preferred_element_type=jnp.float32,
    )


def matmul(left, right):
    return jnp.dot(left, right, precision=lax.Precision.HIGHEST, preferred_element_type=jnp.float32)


def on_device(snapshots, space_factor):
    projected = lax.psum(matmul(snapshots, space_factor), "space")
    devices = lax.axis_size("tm")
    scaling = jnp.float32(math.sqrt(devices * snapshots.shape[0]))
    energy = lax.psum(jnp.sum(projected * projected), "tm")
    factor = projected / jnp.sqrt(energy)
    identity_mat = jnp.eye(RANK, dtype=jnp.float32)

    def advance(sweep, current):
        correlation = lax.psum(inner(current, current), "tm")
        return matmul(current, 1.5 * identity_mat - 0.5 * correlation)

    factor = lax.fori_loop(0, NS, advance, factor)
    loadings = lax.psum_scatter(inner(factor, snapshots), "tm", scatter_dimension=0, tiled=True)
    return (factor * scaling, loadings)


def solution(mesh):
    return jax.shard_map(
        on_device,
        mesh=mesh,
        in_specs=(P("tm", "space"), P("space", None)),
        out_specs=(P("tm", None), P("tm", "space")),
        check_vma=False,
    )
```

profile of v0, /device:TPU:8, one launch (start us, length us, event | category | flops | bytes accessed | tf_op | source)
XLA Modules:
  0.0 756.8 jit_solution(8482115746510413596)
XLA Ops:
  7.2 0.0 copy-start
  7.2 0.0 all-reduce.5.cloned.1.call-start
  7.2 1.2 copy-done
  8.4 5.1 fusion.10
  13.5 0.0 all-reduce.5.cloned.1.call-update
  13.5 48.2 %all-reduce.5.cloned.1.call-done = f32[64,256]{1,0:T(8,128)} async-done(((f32[64,256]{1,0:T(8,128)}), f32[64,256]{1,0:T(8,128)}) %all-reduce.5.cloned.1.call-update) | async-done | bytes 65552 | tf_op jit(solution)/shard_map/psum | solution.py:26
  61.7 1.5 multiply_reduce_fusion
  63.1 127.8 %psum.22 = f32[]{:T(128)} all-reduce(f32[]{:T(128)} %multiply_reduce_fusion), channel_id=1, replica_groups=mesh['tm'=64,'space'=4] {'tm'}, use_global_device_ids=true, to_apply=%region_2.0 | all-reduce | flops 1 | bytes 8 | tf_op jit(solution)/shard_map/psum | solution.py:29
  191.6 0.9 broadcast_divide_fusion
  192.5 356.2 %while.11 = (s32[]{:T(128)}, f32[64,256]{1,0:T(8,128)S(1)}, s32[]{:T(128)}) while((s32[]{:T(128)}, f32[64,256]{1,0:T(8,128)S(1)}, s32[]{:T(128)}) %tuple.25), condition=%wide.region_5.0_spmd.clone, body=%wide.region_3.0_spmd.clone.sunk | while | flops 100990976 | bytes 2424917 | solution.py:37
  192.5 0.0 all-reduce.9.cloned.1.call-start
  192.5 1.1 fusion.26
  193.7 0.0 all-reduce.9.cloned.1.call-update
  193.7 173.3 %all-reduce.9.cloned.1.call-done = f32[256,256]{1,0:T(8,128)} async-done(((f32[256,256]{1,0:T(8,128)}), f32[256,256]{1,0:T(8,128)}) %all-reduce.9.cloned.1.call-update) | async-done | bytes 262160 | tf_op jit(solution)/shard_map/while/body/eval_jaxpr/psum | solution.py:34
  366.9 1.3 convolution_bitcast_fusion.2
  368.2 0.0 all-reduce.9.cloned.1.call-start
  368.3 1.1 fusion.26
  369.4 0.0 all-reduce.9.cloned.1.call-update
  369.4 178.0 %all-reduce.9.cloned.1.call-done = f32[256,256]{1,0:T(8,128)} async-done(((f32[256,256]{1,0:T(8,128)}), f32[256,256]{1,0:T(8,128)}) %all-reduce.9.cloned.1.call-update) | async-done | bytes 262160 | tf_op jit(solution)/shard_map/while/body/eval_jaxpr/psum | solution.py:34
  547.4 1.3 convolution_bitcast_fusion.2
  548.7 0.0 all-reduce.7.cloned.1.call-start
  548.8 0.0 copy-start.1
  548.8 5.1 fusion.11
  553.9 0.0 all-reduce.7.cloned.1.call-update
  553.9 0.0 copy-done.1
  553.9 0.6 dynamic-slice
  555.2 0.6 broadcast_multiply_fusion
  555.8 192.9 %all-reduce.7.cloned.1.call-done = f32[256,4096]{1,0:T(8,128)} async-done(((f32[256,4096]{1,0:T(8,128)}), f32[256,4096]{1,0:T(8,128)}) %all-reduce.7.cloned.1.call-update) | async-done | bytes 4194320
  748.8 1.5 constant_dynamic-slice_fusion
  (2 shorter events, 0.0 us)
Async XLA Ops:
  7.2 1.2 copy-start
  7.2 54.5 %all-reduce.5.cloned.1.call-start = ((), (), s32[]{:S(2)}) async-start(), calls=%async_computation | async-start | bytes 131072 | tf_op jit(solution)/shard_map/psum | solution.py:26
  192.5 174.5 %all-reduce.9.cloned.1.call-start = ((), (), s32[]{:S(2)}) async-start(), calls=%async_computation.2 | async-start | bytes 524288 | tf_op jit(solution)/shard_map/while/body/eval_jaxpr/psum | solution.py:34
  368.2 179.2 %all-reduce.9.cloned.1.call-start = ((), (), s32[]{:S(2)}) async-start(), calls=%async_computation.2 | async-start | bytes 524288 | tf_op jit(solution)/shard_map/while/body/eval_jaxpr/psum | solution.py:34
  548.7 200.0 %all-reduce.7.cloned.1.call-start = ((), (), s32[]{:S(2)}) async-start(), calls=%async_computation.1 | async-start | bytes 8388608
  548.8 5.2 copy-start.1
Sparse Core Ops, SparseCore 0:
  13.6 48.0 all-reduce.4
  196.8 170.1 all-reduce.8
  372.5 174.8 all-reduce.8
  554.1 194.6 all-reduce.6
where the time goes:
time: 757 us
  waiting for transfers between devices  592 us (78%)
  blocking collectives  128 us (17%)
  between operations  15.1 us (2%)
  matrix products  15 us (2%)
    psum x2, waiting for transfers between devices, advance(): correlation = lax.psum(inner(current, current), 'tm')  351 us
    unnamed x3, waiting for transfers between devices  193 us
    psum x1, blocking collectives, on_device(): energy = lax.psum(jnp.sum(projected * projected), 'tm')  128 us
    psum x1, waiting for transfers between devices, on_device(): projected = lax.psum(matmul(snapshots, space_factor), 'space')  48.2 us
  transfers between devices with their start and end apart: 4, of which 4 were waited for; matrix products, arithmetic and copies ran while one was open for 0% of the time, Pallas kernels for 0%

commit v1 on v0

--- a/solution.py
+++ b/solution.py
@@ -23,7 +23,9 @@
 
 
 def on_device(snapshots, space_factor):
-    projected = lax.psum(matmul(snapshots, space_factor), "space")
+    own = matmul(snapshots, space_factor)
+    parts = lax.all_gather(own, "space")
+    projected = jnp.sum(parts, axis=0)
     devices = lax.axis_size("tm")
     scaling = jnp.float32(math.sqrt(devices * snapshots.shape[0]))
     energy = lax.psum(jnp.sum(projected * projected), "tm")

time: 757 us -> 722 us (0.954)
  waiting for transfers between devices: 592 us -> 543 us
  blocking collectives: 128 us -> 142 us
    psum x1 -> x0, waiting for transfers between devices: 48.2 us -> none  [on_device(): projected = lax.psum(matmul(snapshots, space_factor), 'space')]
    all_gather x0 -> x1, blocking collectives: none -> 12.5 us  [on_device(): parts = lax.all_gather(own, 'space')]
    unnamed x3 -> x2, waiting for transfers between devices: 193 us -> 193 us
  transfers between devices with their start and end apart: 4 -> 3, of which waited for: 4 -> 3; matrix products, arithmetic and copies ran while one was open for 0% -> 0% of each run, Pallas kernels for 0% -> 0%
where the time goes in v1:
time: 722 us; the launch traced here: 721 us
  waiting for transfers between devices  543 us (75%)
  blocking collectives  142 us (20%)
  between operations  16.8 us (2%)
  matrix products  14.3 us (2%)
    psum x2, waiting for transfers between devices, advance(): correlation = lax.psum(inner(current, current), 'tm')  351 us
    unnamed x2, waiting for transfers between devices  193 us
    psum x1, blocking collectives, on_device(): energy = lax.psum(jnp.sum(projected * projected), 'tm')  129 us
  transfers between devices with their start and end apart: 3, of which 3 were waited for; matrix products, arithmetic and copies ran while one was open for 0% of the time, Pallas kernels for 0%

profile of v1, /device:TPU:8, one launch (start us, length us, event | category | flops | bytes accessed | tf_op | source)
XLA Modules:
  0.0 721.2 jit_solution(15980828880150380366)
XLA Ops:
  8.0 0.0 copy-start
  8.0 1.2 copy-done
  9.2 4.4 fusion.10
  13.7 12.5 %all-gather = f32[256,256]{1,0:T(8,128)S(1)} all-gather(f32[64,256]{1,0:T(8,128)S(1)} %fusion.10), channel_id=2, replica_groups=mesh['tm'=64,'space'=4] {'space'}, dimensions={0}, use_global_device_ids=true | all-gather | bytes 327680 | tf_op jit(solution)/shard_map/all_gather | solution.py:27
  26.2 0.6 multiply_reduce_fusion
  26.8 129.2 %psum.14 = f32[]{:T(128)} all-reduce(f32[]{:T(128)} %multiply_reduce_fusion), channel_id=1, replica_groups=mesh['tm'=64,'space'=4] {'tm'}, use_global_device_ids=true, to_apply=%region_2.0 | all-reduce | flops 1 | bytes 8 | tf_op jit(solution)/shard_map/psum | solution.py:31
  156.7 355.6 %while.11 = (s32[]{:T(128)}, f32[64,256]{1,0:T(8,128)S(1)}, s32[]{:T(128)}) while((s32[]{:T(128)}, f32[64,256]{1,0:T(8,128)S(1)}, s32[]{:T(128)}) %tuple.25), condition=%wide.region_5.0_spmd.clone, body=%wide.region_3.0_spmd.clone.sunk | while | flops 100990976 | bytes 2424917 | solution.py:39
  156.8 0.0 all-reduce.6.cloned.1.call-start
  156.8 1.1 fusion.26
  157.9 0.0 all-reduce.6.cloned.1.call-update
  158.0 172.7 %all-reduce.6.cloned.1.call-done = f32[256,256]{1,0:T(8,128)} async-done(((f32[256,256]{1,0:T(8,128)}), f32[256,256]{1,0:T(8,128)}) %all-reduce.6.cloned.1.call-update) | async-done | bytes 262160 | tf_op jit(solution)/shard_map/while/body/eval_jaxpr/psum | solution.py:36
  330.6 1.3 convolution_bitcast_fusion.2
  331.9 0.0 all-reduce.6.cloned.1.call-start
  332.0 1.1 fusion.26
  333.1 0.0 all-reduce.6.cloned.1.call-update
  333.1 178.0 %all-reduce.6.cloned.1.call-done = f32[256,256]{1,0:T(8,128)} async-done(((f32[256,256]{1,0:T(8,128)}), f32[256,256]{1,0:T(8,128)}) %all-reduce.6.cloned.1.call-update) | async-done | bytes 262160 | tf_op jit(solution)/shard_map/while/body/eval_jaxpr/psum | solution.py:36
  511.1 1.3 convolution_bitcast_fusion.2
  512.4 0.0 all-reduce.4.cloned.1.call-start
  512.4 0.0 copy-start.1
  512.5 5.1 fusion.11
  517.6 0.0 all-reduce.4.cloned.1.call-update
  517.6 0.0 copy-done.1
  517.6 0.6 dynamic-slice
  518.9 0.6 broadcast_multiply_fusion
  519.5 192.7 %all-reduce.4.cloned.1.call-done = f32[256,4096]{1,0:T(8,128)} async-done(((f32[256,4096]{1,0:T(8,128)}), f32[256,4096]{1,0:T(8,128)}) %all-reduce.4.cloned.1.call-update) | async-done | bytes 4194320
  712.2 1.5 constant_dynamic-slice_fusion
  (4 shorter events, 0.0 us)
Async XLA Ops:
  8.0 1.2 copy-start
  156.8 173.9 %all-reduce.6.cloned.1.call-start = ((), (), s32[]{:S(2)}) async-start(), calls=%async_computation.1 | async-start | bytes 524288 | tf_op jit(solution)/shard_map/while/body/eval_jaxpr/psum | solution.py:36
  331.9 179.2 %all-reduce.6.cloned.1.call-start = ((), (), s32[]{:S(2)}) async-start(), calls=%async_computation.1 | async-start | bytes 524288 | tf_op jit(solution)/shard_map/while/body/eval_jaxpr/psum | solution.py:36
  512.4 199.8 %all-reduce.4.cloned.1.call-start = ((), (), s32[]{:S(2)}) async-start(), calls=%async_computation | async-start | bytes 8388608
  512.4 5.2 copy-start.1
Sparse Core Ops, SparseCore 0:
  161.0 169.5 all-reduce.5
  336.2 174.8 all-reduce.5
Sparse Core Ops, SparseCore 1:
  517.7 194.4 all-reduce.3
